TPU v7x, 32 devices: a whole 2x2x4 slice. The times are simulated.
32 devices in a mesh: fields: 2 (over y), rows: 4 (over z), cols: 2 (over x), sub: 2 (over core).
Axes of the slice: x: 2, y: 2, z: 4, core: 2. Of those that a mesh axis runs over, the one named last changes fastest.
Arguments:
- convergence: bfloat16 [32, 32, 16, 512], P(('fields', 'rows'), 'cols'), parts along dimension 0, may hold values from -6 to 6
- block_level: int32 [32, 32], P(('fields', 'rows'), 'cols'), parts along dimension 0, may hold values from 0 to 1
- near_codes: int32 [32, 32, 8], P(('fields', 'rows'), 'cols', 'sub'), parts along dimension 0, may hold values from 0 to 24, as said below
- far_rows: int32 [32, 32, 4], P(('fields', 'rows'), 'cols', 'sub'), parts along dimension 0, may hold values from 0 to 15, as said below
- near_factor: bfloat16 [512, 4096], P(None, 'sub'), may hold values from -0.09375 to 0.09375
- far_factor: bfloat16 [512, 2048], P(None, 'sub'), may hold values from -0.125 to 0.125
Outputs:
- whitened: bfloat16 [32, 32, 16, 512], P(('fields', 'rows'), 'cols', 'sub'), parts along dimension 0
There are 2 independent parts, one for each index of `fields`. A program takes and returns all parts, laid end to end along the dimension named above; an argument that names none is the same for every part. Nothing has to cross between parts.
Inputs may be any that keep to these rules, and one draw needn't show every extreme that they name: `near_codes`: the 8 codes of a block are different from one another and never 12 (the block itself). `far_rows`: an entry never names a block row held by the same index of rows as the block. Among the 128 entries that one index of rows, cols and sub holds (slots 0 to 1 or 2 to 3), each other index of rows is named at most 64 times through its block rows, and one is named exactly 64 times.
All inputs are finite; a program needn't handle non-finite values.
Results may differ from a plain program's by a relative error of at most 0.001.
Values may be sent and summed in bfloat16 or wider, within the bound.
A program may use at most 64 MiB of HBM per device.

v0:
```python
import functools

import jax
import jax.numpy as jnp
from jax import lax
from jax.experimental import pallas as pl
from jax.experimental.pallas import tpu as pltpu
from jax.sharding import PartitionSpec as P

MESH = pl.DeviceIdType.MESH
PARTS = 4


def chunk_starts(cols):
    return [0, cols * 5 // 16, cols * 10 // 16, cols * 14 // 16, cols]


def kernel(dims, conv, codes, near_factor, far_factor, out, *scratch):
    n_rows, n_cols, tile_rows, tile_cols, half, pixels, near_slots, far_slots = dims
    starts = chunk_starts(tile_cols)
    chunks = len(starts) - 1
    sizes = [starts[k + 1] - starts[k] for k in range(chunks)]
    far = scratch[:chunks]
    (near, near_w, far_w, codes_v, codes_s, near_g, far_g, near_acc, far_acc, end_acc,
     white_src, white_dst, tile_send, tile_recv, white_send, white_recv,
     side_send, side_recv, corner_send, corner_recv, code_send, code_recv, fac_send, fac_recv, loc_sem, halo_sem) = scratch[chunks:]

    i = lax.axis_index("rows")
    x = lax.axis_index("cols")
    s = lax.axis_index("sub")
    other = 1 - s
    mine = pl.ds(pl.multiple_of(s * half, half), half)
    is_end = (i == 0) | (i == n_rows - 1)
    is_mid = (i > 0) & (i < n_rows - 1)
    low_helper = i == 1
    high_helper = i == n_rows - 2
    is_helper = low_helper | high_helper
    end_tile = jnp.where(low_helper, 0, n_rows - 1)
    to_mid = jnp.where(i == 0, 1, n_rows - 2)

    def cols_of(k):
        return pl.ds(starts[k], sizes[k])

    local = [
        pltpu.make_async_copy(
            conv.at[:, :, mine, :],
            near.at[pl.ds(2, tile_rows), pl.ds(2, tile_cols)],
            loc_sem.at[0],
        ),
        pltpu.make_async_copy(near_factor, near_w.at[s], loc_sem.at[1]),
        pltpu.make_async_copy(far_factor, far_w.at[s], loc_sem.at[2]),
        pltpu.make_async_copy(codes, codes_s.at[0, s], loc_sem.at[3]),
    ]
    for copy in local:
        copy.start()
    own_far = [
        pltpu.make_async_copy(
            conv.at[:, cols_of(k), mine, :],
            far[k].at[pl.ds(i * tile_rows, tile_rows)],
            loc_sem.at[6 + k],
        )
        for k in range(chunks)
    ]

    @pl.when(is_mid)
    def _():
        for copy in own_far:
            copy.start()

    @pl.when(i == 0)
    def _():
        near[0:2] = jnp.zeros((2,) + near.shape[1:], near.dtype)

    @pl.when(i == n_rows - 1)
    def _():
        near[tile_rows + 2:tile_rows + 4] = jnp.zeros((2,) + near.shape[1:], near.dtype)

    @pl.when(x == 0)
    def _():
        near[:, 0:2] = jnp.zeros((near.shape[0], 2) + near.shape[2:], near.dtype)

    @pl.when(x == n_cols - 1)
    def _():
        near[:, tile_cols + 2:tile_cols + 4] = jnp.zeros((near.shape[0], 2) + near.shape[2:], near.dtype)

    barrier = pltpu.get_barrier_semaphore()
    offsets = [(-1, 0), (1, 0), (0, -1), (0, 1)]

    def present(di, dx):
        ok = jnp.bool_(True)
        if di == -1:
            ok = ok & (i > 0)
        if di == 1:
            ok = ok & (i < n_rows - 1)
        if dx == -1:
            ok = ok & (x > 0)
        if dx == 1:
            ok = ok & (x < n_cols - 1)
        return ok

    for di, dx in offsets:
        @pl.when(present(di, dx))
        def _():
            pl.semaphore_signal(barrier, inc=1, device_id={"rows": i + di, "cols": x + dx}, device_id_type=MESH)
    pl.semaphore_signal(barrier, inc=1, device_id={"sub": other}, device_id_type=MESH)
    count_z = (i > 0).astype(jnp.int32) + (i < n_rows - 1).astype(jnp.int32)
    count_x = (x > 0).astype(jnp.int32) + (x < n_cols - 1).astype(jnp.int32)
    pl.semaphore_wait(barrier, count_z + count_x + 1)

    def code_copy(which, slot, target):
        return pltpu.make_async_remote_copy(
            src_ref=codes if which < 2 else codes_v.at[slot, s], dst_ref=codes_v.at[slot, s],
            send_sem=code_send.at[which], recv_sem=code_recv.at[which], device_id=target, device_id_type=MESH)

    code_partner = code_copy(0, 0, {"sub": other})
    code_straight = code_copy(1, 1, {"rows": to_mid})
    code_relay = code_copy(2, 1, {"sub": other})
    code_partner.start()

    @pl.when(is_end)
    def _():
        code_straight.start()

    def side_copy(di, dx):
        if di == 0:
            rows_src, rows_dst = pl.ds(0, tile_rows), pl.ds(2, tile_rows)
        elif di == -1:
            rows_src, rows_dst = pl.ds(0, 2), pl.ds(tile_rows + 2, 2)
        else:
            rows_src, rows_dst = pl.ds(tile_rows - 2, 2), pl.ds(0, 2)
        if dx == 0:
            cols_src, cols_dst = pl.ds(0, tile_cols), pl.ds(2, tile_cols)
        elif dx == -1:
            cols_src, cols_dst = pl.ds(0, 2), pl.ds(tile_cols + 2, 2)
        else:
            cols_src, cols_dst = pl.ds(tile_cols - 2, 2), pl.ds(0, 2)
        which = offsets.index((di, dx))
        return pltpu.make_async_remote_copy(
            src_ref=conv.at[rows_src, cols_src, mine, :],
            dst_ref=near.at[rows_dst, cols_dst],
            send_sem=side_send.at[which], recv_sem=side_recv.at[which],
            device_id={"rows": i + di, "cols": x + dx}, device_id_type=MESH)

    def side_sends(di, dx):
        if dx == 0:
            return low_helper if di == -1 else high_helper
        return present(di, dx)

    def side_receives(di, dx):
        if dx == 0:
            return (i == 0) if di == -1 else (i == n_rows - 1)
        return present(-di, -dx)

    def tile_copy(way, d, k, tile):
        src = conv.at[:, cols_of(k), mine, :] if d == 0 else far[k].at[pl.ds(tile * tile_rows, tile_rows)]
        return pltpu.make_async_remote_copy(
            src_ref=src, dst_ref=far[k].at[pl.ds(tile * tile_rows, tile_rows)],
            send_sem=tile_send.at[way, d, k], recv_sem=tile_recv.at[way, d, k],
            device_id={"rows": i - 1 if way == 0 else i + 1}, device_id_type=MESH)

    def sent(way, d, k):
        return tile_copy(way, d, k, i + d if way == 0 else i - d)

    def received(way, d, k):
        return tile_copy(way, d, k, i + 1 + d if way == 0 else i - 1 - d)

    def tile_sends(way, d):
        if way == 0:
            return (i >= 2) & (i + d <= n_rows - 1)
        return (i <= n_rows - 3) & (i - d >= 0)

    def tile_receives(way, d):
        if way == 0:
            return is_mid & (i + 1 + d <= n_rows - 1)
        return is_mid & (i - 1 - d >= 0)

    for k in range(chunks):
        for way in (0, 1):
            @pl.when(tile_sends(way, 0))
            def _():
                sent(way, 0, k).start()
        if k == 0:
            for di, dx in offsets:
                @pl.when(side_sends(di, dx))
                def _():
                    side_copy(di, dx).start()

    def factor_copy(which):
        src, dst = ((near_factor, near_w), (far_factor, far_w))[which]
        return pltpu.make_async_remote_copy(
            src_ref=src, dst_ref=dst.at[s], send_sem=fac_send.at[which],
            recv_sem=fac_recv.at[which], device_id={"sub": other}, device_id_type=MESH)

    for which in (0, 1):
        factor_copy(which).start()

    def halo_copy(way, k):
        if way == 0:
            src_rows, dst_rows = pl.ds((i + 1) * tile_rows, 2), pl.ds(tile_rows + 2, 2)
        else:
            src_rows, dst_rows = pl.ds(i * tile_rows - 2, 2), pl.ds(0, 2)
        return pltpu.make_async_copy(
            far[k].at[src_rows], near.at[dst_rows, pl.ds(2 + starts[k], sizes[k])], halo_sem.at[way, k])

    for d in range(n_rows - 3):
        for k in range(chunks):
            for way in (0, 1):
                @pl.when(tile_receives(way, d))
                def _():
                    received(way, d, k).wait_recv()
                    if d == 0:
                        halo_copy(way, k).start()

                @pl.when(tile_sends(way, d + 1))
                def _():
                    sent(way, d + 1, k).start()

    code_copy(0, 0, {"sub": other}).wait_recv()
    code_in = pltpu.make_async_copy(codes_v.at[0, other], codes_s.at[0, other], loc_sem.at[4])
    code_in.start()
    end_codes = pltpu.make_async_copy(codes_v.at[1], codes_s.at[1], loc_sem.at[5])

    @pl.when(is_helper)
    def _():
        code_straight.wait_recv()
        code_relay.start()

    for copy in local:
        copy.wait()

    @pl.when(is_mid)
    def _():
        for k in range(chunks):
            halo_copy(0, k).wait()
            halo_copy(1, k).wait()
            own_far[k].wait()

    for di, dx in offsets:
        @pl.when(side_receives(di, dx))
        def _():
            side_copy(di, dx).wait_recv()

    def corner_copy(di, dx):
        rows = pl.ds(0, 2) if di == -1 else pl.ds(tile_rows + 2, 2)
        src, dst = (2, tile_cols + 2) if dx == -1 else (tile_cols, 0)
        which = (di + 1) + (dx + 1) // 2
        return pltpu.make_async_remote_copy(
            src_ref=near.at[rows, pl.ds(src, 2)], dst_ref=near.at[rows, pl.ds(dst, 2)],
            send_sem=corner_send.at[which], recv_sem=corner_recv.at[which],
            device_id={"cols": x + dx}, device_id_type=MESH)

    corners = [(di, dx) for di in (-1, 1) for dx in (-1, 1)]
    for di, dx in corners:
        @pl.when(present(di, 0) & present(0, dx))
        def _():
            corner_copy(di, dx).start()

    @pl.when(is_helper)
    def _():
        code_relay.wait_recv()
        end_codes.start()
        end_codes.wait()

    code_in.wait()
    for which in (0, 1):
        factor_copy(which).wait_recv()
    for di, dx in corners:
        @pl.when(present(di, 0) & present(0, -dx))
        def _():
            corner_copy(di, dx).wait_recv()

    contract = (((1,), (1,)), ((), ()))
    part_slots = 2 * near_slots // PARTS

    def block_rows(block):
        return pl.ds(pl.multiple_of(block * half, half), half)

    def pair_rows(block):
        return pl.ds(pl.multiple_of(block * half, 2 * half), 2 * half)

    def joined(first, second):
        both = jnp.concatenate([first.astype(jnp.float32), second.astype(jnp.float32)], axis=0)
        return both.astype(jnp.bfloat16)

    def near_part(part):
        sub, base = part * part_slots // near_slots, part * part_slots % near_slots

        def near_block(r, c, slot):
            code = codes_s[0, sub, r, base + slot, c]
            down = lax.shift_right_logical(code * 205, 10)
            return near[r + down, c + code - 5 * down]

        def gather(c, carry):
            for r in range(0, tile_rows, 2):
                for slot in range(part_slots):
                    near_g[pair_rows(c * tile_rows + r), slot * pixels:(slot + 1) * pixels] = joined(
                        near_block(r, c, slot), near_block(r + 1, c, slot))
            return carry

        lax.fori_loop(0, tile_cols, gather, 0)
        product = lax.dot_general(
            near_g[...], near_w[sub, :, base * pixels:(base + part_slots) * pixels], contract,
            preferred_element_type=jnp.float32)
        if part == 0:
            near_acc[...] = product
        else:
            near_acc[...] += product

    level_at = near_slots + far_slots

    def far_chunk(k):
        rows = sizes[k] * tile_rows * half

        def gather_far(who):
            def far_block(r, c, sub, slot):
                row = codes_s[who, sub, r, near_slots + slot, starts[k] + c]
                return far[k][row, c]

            def body(c, carry):
                for r in range(0, tile_rows, 2):
                    for sub in range(2):
                        for slot in range(far_slots):
                            at = sub * far_slots + slot
                            far_g[pair_rows((who * sizes[k] + c) * tile_rows + r), at * pixels:(at + 1) * pixels] = joined(
                                far_block(r, c, sub, slot), far_block(r + 1, c, sub, slot))
                return carry

            lax.fori_loop(0, sizes[k], body, 0)

        gather_far(0)

        @pl.when(is_helper)
        def _():
            gather_far(1)

        depth = far_slots * pixels
        product = lax.dot_general(
            far_g[:2 * rows, :depth], far_w[0], contract, preferred_element_type=jnp.float32)
        product += lax.dot_general(
            far_g[:2 * rows, depth:], far_w[1], contract, preferred_element_type=jnp.float32)
        far_acc[pl.ds(starts[k] * tile_rows * half, rows), :] = product[:rows]
        end_acc[pl.ds(0, rows), :] = product[rows:]

        @pl.when(is_helper)
        def _():
            def body(c, carry):
                for r in range(tile_rows):
                    value = far[k][end_tile * tile_rows + r, c].astype(jnp.float32)
                    white_src[r, starts[k] + c] = (value - end_acc[block_rows(c * tile_rows + r), :]).astype(jnp.bfloat16)
                return carry

            lax.fori_loop(0, sizes[k], body, 0)
            white_copy(k).start()

    def white_copy(k):
        return pltpu.make_async_remote_copy(
            src_ref=white_src.at[:, cols_of(k)], dst_ref=white_dst.at[:, cols_of(k)],
            send_sem=white_send.at[k], recv_sem=white_recv.at[k],
            device_id={"rows": end_tile}, device_id_type=MESH)

    @pl.when(is_mid)
    def _():
        near_part(0)
        for k in range(chunks):
            d = n_rows - 3
            for way in (0, 1):
                @pl.when(tile_receives(way, d))
                def _():
                    received(way, d, k).wait_recv()
            far_chunk(k)
            if k < PARTS - 2:
                near_part(k + 1)
        near_part(PARTS - 1)

        def body(c, carry):
            for r in range(tile_rows):
                level = codes_s[0, s, r, level_at, c]
                at = block_rows(c * tile_rows + r)
                mean = jnp.where(level == 1, near_acc[at, :], far_acc[at, :])
                out[r, c] = (near[2 + r, 2 + c].astype(jnp.float32) - mean).astype(jnp.bfloat16)
            return carry

        lax.fori_loop(0, tile_cols, body, 0)

    @pl.when(is_end)
    def _():
        for part in range(PARTS):
            near_part(part)
        for k in range(chunks):
            white_copy(k).wait_recv()

            def body(c, carry):
                for r in range(tile_rows):
                    level = codes_s[0, s, r, level_at, c]
                    mean = near_acc[block_rows(c * tile_rows + r), :]
                    fine = near[2 + r, 2 + c].astype(jnp.float32) - mean
                    coarse = white_dst[r, c].astype(jnp.float32)
                    out[r, c] = jnp.where(level == 1, fine, coarse).astype(jnp.bfloat16)
                return carry

            lax.fori_loop(starts[k], starts[k + 1], body, 0)

    code_partner.wait_send()

    @pl.when(is_end)
    def _():
        code_straight.wait_send()

    for di, dx in corners:
        @pl.when(present(di, 0) & present(0, dx))
        def _():
            corner_copy(di, dx).wait_send()

    for di, dx in offsets:
        @pl.when(side_sends(di, dx))
        def _():
            side_copy(di, dx).wait_send()
    for which in (0, 1):
        factor_copy(which).wait_send()
    for d in range(n_rows - 2):
        for way in (0, 1):
            @pl.when(tile_sends(way, d))
            def _():
                for k in range(chunks):
                    sent(way, d, k).wait_send()

    @pl.when(is_helper)
    def _():
        code_relay.wait_send()
        for k in range(chunks):
            white_copy(k).wait_send()


def on_device(convergence, block_level, near_codes, far_rows, near_factor, far_factor):
    tile_rows, tile_cols, samples, pixels = convergence.shape
    n_rows, n_cols = lax.axis_size("rows"), lax.axis_size("cols")
    near_slots, far_slots = near_codes.shape[2], far_rows.shape[2]
    half = samples // 2
    starts = chunk_starts(tile_cols)
    chunks = len(starts) - 1
    codes = jnp.concatenate(
        [jnp.transpose(near_codes, (0, 2, 1)), jnp.transpose(far_rows, (0, 2, 1)), block_level[:, None, :]], axis=1)
    dims = (n_rows, n_cols, tile_rows, tile_cols, half, pixels, near_slots, far_slots)
    block = (half, pixels)
    bf16, f32 = jnp.bfloat16, jnp.float32
    all_rows = tile_rows * tile_cols * half
    chunk_rows = tile_rows * half * max(starts[k + 1] - starts[k] for k in range(chunks))
    dma = pltpu.SemaphoreType.DMA
    scratch = [pltpu.VMEM((n_rows * tile_rows, starts[k + 1] - starts[k]) + block, bf16) for k in range(chunks)]
    scratch += [
        pltpu.VMEM((tile_rows + 4, tile_cols + 4) + block, bf16),
        pltpu.VMEM((2,) + near_factor.shape, bf16),
        pltpu.VMEM((2,) + far_factor.shape, bf16),
        pltpu.VMEM((2, 2) + codes.shape, jnp.int32),
        pltpu.SMEM((2, 2) + codes.shape, jnp.int32),
        pltpu.VMEM((all_rows, 2 * near_slots // PARTS * pixels), bf16),
        pltpu.VMEM((2 * chunk_rows, 2 * far_slots * pixels), bf16),
        pltpu.VMEM((all_rows, pixels), f32),
        pltpu.VMEM((all_rows, pixels), f32),
        pltpu.VMEM((chunk_rows, pixels), f32),
        pltpu.VMEM((tile_rows, tile_cols) + block, bf16),
        pltpu.VMEM((tile_rows, tile_cols) + block, bf16),
        dma((2, n_rows - 2, chunks)),
        dma((2, n_rows - 2, chunks)),
        dma((chunks,)),
        dma((chunks,)),
        dma((4,)),
        dma((4,)),
        dma((4,)),
        dma((4,)),
        dma((3,)),
        dma((3,)),
        dma((2,)),
        dma((2,)),
        dma((6 + chunks,)),
        dma((2, chunks)),
    ]
    anywhere = pl.BlockSpec(memory_space=pl.ANY)
    vmem = pl.BlockSpec(memory_space=pltpu.VMEM)
    return pl.pallas_call(
        functools.partial(kernel, dims),
        out_shape=jax.ShapeDtypeStruct((tile_rows, tile_cols) + block, bf16),
        in_specs=[anywhere, vmem, anywhere, anywhere],
        out_specs=vmem,
        scratch_shapes=scratch,
        compiler_params=pltpu.CompilerParams(
            collective_id=0, has_side_effects=True, vmem_limit_bytes=56 * 1024 * 1024),
    )(convergence, codes, near_factor, far_factor)


def solution(mesh):
    placed = (
        P(("fields", "rows"), "cols", None, None),
        P(("fields", "rows"), "cols"),
        P(("fields", "rows"), "cols", "sub"),
        P(("fields", "rows"), "cols", "sub"),
        P(None, "sub"),
        P(None, "sub"),
    )
    return jax.shard_map(
        on_device,
        mesh=mesh,
        in_specs=placed,
        out_specs=P(("fields", "rows"), "cols", "sub", None),
        check_vma=False,
    )
```

profile of v0, /device:TPU:0, one launch (start us, length us, event | category | flops | bytes accessed | tf_op | source)
XLA Modules:
  0.0 42.1 jit_solution(16879331448474158465)
XLA Ops:
  0.0 1.3 %pad_add_fusion.codes = s32[4,7,16]{2,1,0:T(8,128)} fusion(s32[4,1,16]{2,1,0:T(1,128)} %bitcast.7, s32[4,2,16]{2,1,0:T(2,128)} %bitcast.6, s32[4,4,16]{2,1,0:T(4,128)} %bitcast.5), kind=kLoop, calls=%fused_computation | loop fusion | flops 896 | bytes 3584 | tf_op jit(solution)/shard_map/concatenate | solution.py:441
  1.3 38.9 %shard_map.64 = bf16[4,16,8,512]{3,2,1,0:T(8,128)(2,1)} custom-call(bf16[4,16,16,512]{3,2,1,0:T(8,128)(2,1)} %conv.1, s32[4,7,16]{2,1,0:T(8,128)} %pad_add_fusion.codes, bf16[512,2048]{1,0:T(8,128)(2,1)} %near_factor.1, bf16[512,1024]{1,0:T(8,128)(2,1)} %far_factor.1), custom_call_target="tpu_custom_call" | custom-call | tf_op jit(solution)/shard_map/pallas_call | solution.py:480
  40.3 1.9 %copy.9 = bf16[4,16,8,512]{3,2,1,0:T(8,128)(2,1)} copy(bf16[4,16,8,512]{3,2,1,0:T(8,128)(2,1)} %shard_map.64) | data formatting | bytes 1048576
where the time goes:
time: 42.4 us; the launch traced here: 42.1 us
  Pallas kernels  38.9 us (92%)
  local copies, waits for them, and re-layouts  1.87 us (4%)
  other arithmetic  1.34 us (3%)
    pallas_call x1, Pallas kernels, on_device(): pl.pallas_call(functools.partial(kernel, dims), out_shape=jax.ShapeDtypeS...  38.9 us
    unnamed x1, local copies, waits for them, and re-layouts  1.87 us
    concatenate x1, other arithmetic, on_device(): jnp.concatenate([jnp.transpose(near_codes, (0, 2, 1)), jnp.transpose(far_...  1.34 us

commit v1 on v0

--- a/solution.py
+++ b/solution.py
@@ -488,6 +488,536 @@
     )(convergence, codes, near_factor, far_factor)
 
 
+def group_starts(cols, served):
+    left = cols - 2 * served
+    return [2 * served, 2 * served + left // 2, 2 * served + left * 3 // 4, cols]
+
+
+def pair_kernel(dims, conv, near_codes, far_codes, levels, near_factor, far_factor, out, *scratch):
+    n_rows, n_cols, tile_rows, tile_cols, half, pixels, near_slots, far_slots, served = dims
+    starts = group_starts(tile_cols, served)
+    chunks = len(starts) - 1
+    sizes = [starts[k + 1] - starts[k] for k in range(chunks)]
+    far_both = scratch[:chunks]
+    (far_served, near, stage, near_w, far_w, near_codes_v, far_codes_v, near_codes_s, far_codes_s, levels_s,
+     near_g, far_g, near_acc, far_acc, white_served, white_both, white_in, send_sem, recv_sem, loc_sem) = scratch[chunks:]
+
+    i = lax.axis_index("rows")
+    x = lax.axis_index("cols")
+    s = lax.axis_index("sub")
+    other = 1 - s
+    mine = pl.ds(pl.multiple_of(s * half, half), half)
+    low = i < n_rows // 2
+    mid = jnp.where(low, n_rows // 2 - 1, n_rows // 2)
+    end = jnp.where(low, 0, n_rows - 1)
+    far_mid, far_end = n_rows - 1 - mid, n_rows - 1 - end
+    is_mid = i == mid
+    is_end = i == end
+    always = i >= 0
+    edge = 2
+    rest = tile_rows - edge
+    in_edge = jnp.where(low, tile_rows - edge, 0)
+    in_rest = jnp.where(low, 0, edge)
+    out_edge = jnp.where(low, 0, tile_rows - edge)
+    below, above = 0, tile_rows + edge
+    served_at = jnp.where(low, 0, served)
+    theirs_at = served - served_at
+    served_cols, theirs_cols = pl.ds(served_at, served), pl.ds(theirs_at, served)
+    inner = pl.ds(edge, tile_cols)
+    count = {"remote": 0, "local": 0}
+
+    class Remote:
+        def __init__(self, sends, receives, src, dst, landed, to):
+            self.at, self.sends, self.receives = count["remote"], sends, receives
+            self.src, self.dst, self.landed, self.to = src, dst, landed, to
+            count["remote"] += 1
+
+        def copy(self, src, dst):
+            return pltpu.make_async_remote_copy(
+                src_ref=src, dst_ref=dst, send_sem=send_sem.at[self.at], recv_sem=recv_sem.at[self.at],
+                device_id=self.to, device_id_type=MESH)
+
+        def start(self):
+            @pl.when(self.sends)
+            def _():
+                self.copy(self.src, self.dst).start()
+
+        def wait_recv(self):
+            @pl.when(self.receives)
+            def _():
+                self.copy(self.landed, self.landed).wait_recv()
+
+        def wait_send(self):
+            @pl.when(self.sends)
+            def _():
+                self.copy(self.src, self.dst).wait_send()
+
+    class Local:
+        def __init__(self, here, src, dst):
+            self.here = here
+            self.copy = pltpu.make_async_copy(src, dst, loc_sem.at[count["local"]])
+            count["local"] += 1
+
+        def start(self):
+            @pl.when(self.here)
+            def _():
+                self.copy.start()
+
+        def wait(self):
+            @pl.when(self.here)
+            def _():
+                self.copy.wait()
+
+    def rows_of(tile, first, size):
+        return pl.ds(tile * tile_rows + first, size)
+
+    def both_cols(k):
+        return pl.ds(starts[k], sizes[k])
+
+    to_partner, to_mid, to_end = {"sub": other}, {"rows": mid}, {"rows": end}
+    to_far_mid, to_far_end = {"rows": far_mid}, {"rows": far_end}
+
+    own = [
+        Local(always, conv.at[:, :, mine, :], near.at[pl.ds(edge, tile_rows), inner]),
+        Local(always, near_factor, near_w.at[s]),
+        Local(is_mid, far_factor, far_w.at[s]),
+        Local(always, near_codes, near_codes_s.at[s]),
+        Local(always, levels, levels_s),
+        Local(is_mid, far_codes, far_codes_s.at[i, s]),
+        Local(is_mid, conv.at[:, served_cols, mine, :], far_served.at[rows_of(i, 0, tile_rows)]),
+    ] + [
+        Local(is_mid, conv.at[:, both_cols(k), mine, :], far_both[k].at[rows_of(i, 0, tile_rows)])
+        for k in range(chunks)
+    ]
+    for copy in own:
+        copy.start()
+
+    def clear(where, rows, cols):
+        @pl.when(where)
+        def _():
+            near[rows, cols] = jnp.zeros((rows.stop - rows.start, cols.stop - cols.start) + near.shape[2:], near.dtype)
+
+    clear(i == 0, slice(0, edge), slice(0, tile_cols + 2 * edge))
+    clear(i == n_rows - 1, slice(above, above + edge), slice(0, tile_cols + 2 * edge))
+    clear(x == 0, slice(0, tile_rows + 2 * edge), slice(0, edge))
+    clear(x == n_cols - 1, slice(0, tile_rows + 2 * edge), slice(tile_cols + edge, tile_cols + 2 * edge))
+
+    def present(di, dx):
+        ok = always
+        if di == -1:
+            ok = ok & (i > 0)
+        if di == 1:
+            ok = ok & (i < n_rows - 1)
+        if dx == -1:
+            ok = ok & (x > 0)
+        if dx == 1:
+            ok = ok & (x < n_cols - 1)
+        return ok
+
+    barrier = pltpu.get_barrier_semaphore()
+    for di, dx in ((-1, 0), (1, 0), (0, -1), (0, 1)):
+        @pl.when(present(di, dx))
+        def _():
+            pl.semaphore_signal(barrier, inc=1, device_id={"rows": i + di, "cols": x + dx}, device_id_type=MESH)
+    pl.semaphore_signal(barrier, inc=1, device_id=to_partner, device_id_type=MESH)
+    count_z = (i > 0).astype(jnp.int32) + (i < n_rows - 1).astype(jnp.int32)
+    count_x = (x > 0).astype(jnp.int32) + (x < n_cols - 1).astype(jnp.int32)
+    pl.semaphore_wait(barrier, count_z + count_x + 1)
+
+    def exchange(src, dst, landed):
+        return Remote(always, always, src, dst, landed, to_partner)
+
+    def inward(src, dst, landed):
+        return Remote(is_end, is_mid, src, dst, landed, to_mid)
+
+    def outward(src, dst, landed):
+        return Remote(is_mid, is_end, src, dst, landed, to_end)
+
+    def across(src, dst, landed):
+        return Remote(is_mid, is_mid, src, dst, landed, to_far_mid)
+
+    def between(src, dst, landed):
+        return Remote(is_mid, is_mid, src, dst, landed, to_partner)
+
+    from_inside = pl.ds(jnp.where(low, above, below), edge)
+    from_outside = pl.ds(jnp.where(low, below, above), edge)
+    edge_rows = conv.at[pl.ds(in_edge, edge), :, mine, :]
+
+    code_near = exchange(near_codes, near_codes_v.at[s], near_codes_v.at[other])
+    code_own = between(far_codes, far_codes_v.at[i, s], far_codes_v.at[i, other])
+    code_end = inward(far_codes, far_codes_v.at[end, s], far_codes_v.at[end, s])
+    code_mid = across(far_codes, far_codes_v.at[mid, s], far_codes_v.at[far_mid, s])
+    code_relay = across(far_codes_v.at[end, s], far_codes_v.at[end, s], far_codes_v.at[far_end, s])
+    code_share = [
+        between(far_codes_v.at[tile, s], far_codes_v.at[tile, s], far_codes_v.at[tile, other])
+        for tile in (end, far_mid, far_end)
+    ]
+
+    mid_edge = across(edge_rows, near.at[from_outside, inner], near.at[from_inside, inner])
+    end_edge = inward(edge_rows, near.at[from_outside, inner], near.at[from_outside, inner])
+    back_edge = outward(
+        conv.at[pl.ds(out_edge, edge), :, mine, :], near.at[from_inside, inner], near.at[from_inside, inner])
+
+    their_rest = pl.ds(jnp.where(low, edge, 0), rest)
+
+    def rest_of(cols):
+        return conv.at[pl.ds(in_rest, rest), cols, mine, :]
+
+    def far_mid_rest(ref):
+        return ref.at[pl.ds(far_mid * tile_rows + jnp.where(low, edge, 0), rest)]
+
+    mid_rest = across(
+        rest_of(theirs_cols), far_served.at[rows_of(mid, in_rest, rest)], far_mid_rest(far_served))
+    mid_rest_both = [
+        across(rest_of(both_cols(k)), far_both[k].at[rows_of(mid, in_rest, rest)], far_mid_rest(far_both[k]))
+        for k in range(chunks)
+    ]
+
+    def end_rest_to(cols, ref):
+        return inward(rest_of(cols), ref, ref)
+
+    end_rest_theirs = end_rest_to(theirs_cols, stage.at[pl.ds(in_rest, rest)])
+    end_rest_both = [
+        end_rest_to(both_cols(k), far_both[k].at[rows_of(end, in_rest, rest)]) for k in range(chunks)
+    ]
+    end_rest_served = end_rest_to(served_cols, far_served.at[rows_of(end, in_rest, rest)])
+
+    relay_theirs = across(
+        stage, far_served.at[rows_of(end, 0, tile_rows)], far_served.at[rows_of(far_end, 0, tile_rows)])
+    relay_both = [
+        across(
+            far_both[k].at[rows_of(end, 0, tile_rows)], far_both[k].at[rows_of(end, 0, tile_rows)],
+            far_both[k].at[rows_of(far_end, 0, tile_rows)])
+        for k in range(chunks)
+    ]
+
+    white_far_end = Remote(
+        is_mid, is_end, white_served.at[2], white_in.at[:, served_cols], white_in.at[:, theirs_cols], to_far_end)
+    white_far_mid = across(white_served.at[1], white_in.at[:, served_cols], white_in.at[:, theirs_cols])
+    white_end = outward(white_served.at[0], white_in.at[:, served_cols], white_in.at[:, served_cols])
+    white_end_both = [
+        outward(
+            white_both.at[:, pl.ds(starts[k] - starts[0], sizes[k])], white_in.at[:, both_cols(k)],
+            white_in.at[:, both_cols(k)])
+        for k in range(chunks)
+    ]
+
+    def side_copy(dx):
+        src, dst = (0, tile_cols + edge) if dx == -1 else (tile_cols - edge, 0)
+        at = near.at[pl.ds(edge, tile_rows), pl.ds(dst, edge)]
+        return Remote(
+            present(0, dx), present(0, -dx), conv.at[:, pl.ds(src, edge), mine, :], at, at, {"cols": x + dx})
+
+    sides = [side_copy(dx) for dx in (-1, 1)]
+
+    def corner_copy(di, dx):
+        rows = pl.ds(below if di == -1 else above, edge)
+        src, dst = (edge, tile_cols + edge) if dx == -1 else (tile_cols, 0)
+        at = near.at[rows, pl.ds(dst, edge)]
+        return Remote(
+            present(di, 0) & present(0, dx), present(di, 0) & present(0, -dx), near.at[rows, pl.ds(src, edge)], at, at,
+            {"cols": x + dx})
+
+    corners = [corner_copy(di, dx) for di in (-1, 1) for dx in (-1, 1)]
+    factor_near = exchange(near_factor, near_w.at[s], near_w.at[other])
+    factor_far = between(far_factor, far_w.at[s], far_w.at[other])
+
+    end_to_far = [
+        Local(is_mid, near.at[from_outside, pl.ds(edge + theirs_at, served)], stage.at[pl.ds(in_edge, edge)]),
+        Local(is_mid, near.at[from_outside, pl.ds(edge + served_at, served)], far_served.at[rows_of(end, in_edge, edge)]),
+    ] + [
+        Local(
+            is_mid, near.at[from_outside, pl.ds(edge + starts[k], sizes[k])],
+            far_both[k].at[rows_of(end, in_edge, edge)])
+        for k in range(chunks)
+    ]
+    their_edge = jnp.where(low, 0, tile_rows - edge)
+    mid_to_far = [
+        Local(
+            is_mid, near.at[from_inside, pl.ds(edge + served_at, served)],
+            far_served.at[pl.ds(far_mid * tile_rows + their_edge, edge)]),
+    ] + [
+        Local(
+            is_mid, near.at[from_inside, pl.ds(edge + starts[k], sizes[k])],
+            far_both[k].at[pl.ds(far_mid * tile_rows + their_edge, edge)])
+        for k in range(chunks)
+    ]
+    near_codes_in = Local(always, near_codes_v.at[other], near_codes_s.at[other])
+    far_codes_in = [Local(is_mid, far_codes_v.at[i, other], far_codes_s.at[i, other])] + [
+        Local(is_mid, far_codes_v.at[tile], far_codes_s.at[tile]) for tile in (end, far_mid, far_end)
+    ]
+
+    first = [code_end, code_mid, code_near, code_own, mid_edge, end_edge, back_edge] + sides + [factor_near, factor_far]
+    for flow in first:
+        flow.start()
+    end_rest_theirs.start()
+    for k in range(chunks):
+        end_rest_both[k].start()
+    end_rest_served.start()
+    code_end.wait_recv()
+    code_relay.start()
+    mid_rest.start()
+    for k in range(chunks):
+        mid_rest_both[k].start()
+    code_share[0].start()
+    code_mid.wait_recv()
+    code_share[1].start()
+    code_near.wait_recv()
+    near_codes_in.start()
+    code_own.wait_recv()
+    far_codes_in[0].start()
+
+    end_edge.wait_recv()
+    for copy in end_to_far:
+        copy.start()
+    mid_edge.wait_recv()
+    back_edge.wait_recv()
+    own[0].wait()
+    for corner in corners:
+        corner.start()
+    for copy in mid_to_far:
+        copy.start()
+    for copy in own[1:]:
+        copy.wait()
+    for copy in end_to_far:
+        copy.wait()
+    end_rest_theirs.wait_recv()
+    relay_theirs.start()
+    near_codes_in.wait()
+    for side in sides:
+        side.wait_recv()
+    factor_near.wait_recv()
+    for corner in corners:
+        corner.wait_recv()
+
+    contract = (((1,), (1,)), ((), ()))
+    part_slots = 2 * near_slots // PARTS
+
+    def block_rows(block):
+        return pl.ds(pl.multiple_of(block * half, half), half)
+
+    def pair_rows(block):
+        return pl.ds(pl.multiple_of(block * half, 2 * half), 2 * half)
+
+    def joined(first, second):
+        both = jnp.concatenate([first.astype(jnp.float32), second.astype(jnp.float32)], axis=0)
+        return both.astype(jnp.bfloat16)
+
+    def near_part(part):
+        sub, base = part * part_slots // near_slots, part * part_slots % near_slots
+
+        def near_block(r, c, slot):
+            code = near_codes_s[sub, r, base + slot, c]
+            down = lax.shift_right_logical(code * 205, 10)
+            return near[r + down, c + code - 5 * down]
+
+        def gather(c, carry):
+            for r in range(0, tile_rows, 2):
+                for slot in range(part_slots):
+                    near_g[pair_rows(c * tile_rows + r), slot * pixels:(slot + 1) * pixels] = joined(
+                        near_block(r, c, slot), near_block(r + 1, c, slot))
+            return carry
+
+        lax.fori_loop(0, tile_cols, gather, 0)
+        product = lax.dot_general(
+            near_g[...], near_w[sub, :, base * pixels:(base + part_slots) * pixels], contract,
+            preferred_element_type=jnp.float32)
+        if part == 0:
+            near_acc[...] = product
+        else:
+            near_acc[...] += product
+
+    def far_group(blocks, col0, size, targets):
+        rows = size * tile_rows * half
+        depth = far_slots * pixels
+
+        def body(c, carry):
+            for who, (tile, _) in enumerate(targets):
+                def far_block(r, sub, slot):
+                    return blocks[far_codes_s[tile, sub, r, slot, col0 + c], c]
+
+                for r in range(0, tile_rows, 2):
+                    for sub in range(2):
+                        for slot in range(far_slots):
+                            at = sub * far_slots + slot
+                            far_g[pair_rows((who * size + c) * tile_rows + r), at * pixels:(at + 1) * pixels] = joined(
+                                far_block(r, sub, slot), far_block(r + 1, sub, slot))
+            return carry
+
+        lax.fori_loop(0, size, body, 0)
+        total = len(targets) * rows
+        product = lax.dot_general(
+            far_g[:total, :depth], far_w[0], contract, preferred_element_type=jnp.float32)
+        product += lax.dot_general(
+            far_g[:total, depth:], far_w[1], contract, preferred_element_type=jnp.float32)
+        far_acc[:total, :] = product
+
+        def subtract(c, carry):
+            for who, (tile, put) in enumerate(targets):
+                for r in range(tile_rows):
+                    value = blocks[tile * tile_rows + r, c].astype(jnp.float32)
+                    put(r, c, value - far_acc[block_rows((who * size + c) * tile_rows + r), :])
+            return carry
+
+        lax.fori_loop(0, size, subtract, 0)
+
+    def fine(r, c):
+        return near[edge + r, edge + c].astype(jnp.float32) - near_acc[block_rows(c * tile_rows + r), :]
+
+    def put_own(col0):
+        def put(r, c, white):
+            out[r, col0 + c] = jnp.where(levels_s[r, col0 + c] == 1, fine(r, col0 + c), white).astype(jnp.bfloat16)
+        return put
+
+    def put_served(which):
+        def put(r, c, white):
+            white_served[which, r, c] = white.astype(jnp.bfloat16)
+        return put
+
+    def put_both(col0):
+        def put(r, c, white):
+            white_both[r, col0 - starts[0] + c] = white.astype(jnp.bfloat16)
+        return put
+
+    def finish(first, last):
+        def body(c, carry):
+            for r in range(tile_rows):
+                white = white_in[r, c].astype(jnp.float32)
+                out[r, c] = jnp.where(levels_s[r, c] == 1, fine(r, c), white).astype(jnp.bfloat16)
+            return carry
+
+        lax.fori_loop(first, last, body, 0)
+
+    @pl.when(is_mid)
+    def _():
+        near_part(0)
+        code_relay.wait_recv()
+        code_share[2].start()
+        near_part(1)
+        for copy in mid_to_far:
+            copy.wait()
+        for k in range(chunks):
+            end_rest_both[k].wait_recv()
+            relay_both[k].start()
+        for k in range(2, PARTS):
+            near_part(k)
+        for share in code_share:
+            share.wait_recv()
+        for copy in far_codes_in[1:]:
+            copy.start()
+        for copy in far_codes_in:
+            copy.wait()
+        factor_far.wait_recv()
+        mid_rest.wait_recv()
+        end_rest_served.wait_recv()
+        relay_theirs.wait_recv()
+        far_group(far_served, served_at, served, [
+            (far_end, put_served(2)), (far_mid, put_served(1)), (end, put_served(0)), (i, put_own(served_at))])
+        white_far_end.start()
+        white_far_mid.start()
+        white_end.start()
+        for k in range(chunks):
+            mid_rest_both[k].wait_recv()
+            relay_both[k].wait_recv()
+            far_group(far_both[k], starts[k], sizes[k], [(end, put_both(starts[k])), (i, put_own(starts[k]))])
+            white_end_both[k].start()
+        white_far_mid.wait_recv()
+        finish(theirs_at, theirs_at + served)
+
+    @pl.when(is_end)
+    def _():
+        for part in range(PARTS):
+            near_part(part)
+        white_end.wait_recv()
+        finish(served_at, served_at + served)
+        for k in range(chunks - 1):
+            white_end_both[k].wait_recv()
+            finish(starts[k], starts[k + 1])
+        white_far_end.wait_recv()
+        finish(theirs_at, theirs_at + served)
+        white_end_both[chunks - 1].wait_recv()
+        finish(starts[chunks - 1], starts[chunks])
+
+    for flow in first + [end_rest_theirs] + end_rest_both + [end_rest_served, code_relay, mid_rest] + mid_rest_both:
+        flow.wait_send()
+    for flow in corners + [relay_theirs] + relay_both + code_share:
+        flow.wait_send()
+    for flow in [white_far_end, white_far_mid, white_end] + white_end_both:
+        flow.wait_send()
+
+
+def put_out(src, dst, sem):
+    pieces = sem.shape[0]
+    size = src.shape[0] // pieces
+    copies = [
+        pltpu.make_async_copy(src.at[pl.ds(k * size, size)], dst.at[pl.ds(k * size, size)], sem.at[k])
+        for k in range(pieces)
+    ]
+    for copy in copies:
+        copy.start()
+    for copy in copies:
+        copy.wait()
+
+
+def pair_on_device(convergence, block_level, near_codes, far_rows, near_factor, far_factor):
+    tile_rows, tile_cols, samples, pixels = convergence.shape
+    n_rows, n_cols = lax.axis_size("rows"), lax.axis_size("cols")
+    near_slots, far_slots = near_codes.shape[2], far_rows.shape[2]
+    half = samples // 2
+    served = tile_cols // 4
+    starts = group_starts(tile_cols, served)
+    sizes = [starts[k + 1] - starts[k] for k in range(len(starts) - 1)]
+    near_codes = jnp.transpose(near_codes, (0, 2, 1))
+    far_codes = jnp.transpose(far_rows, (0, 2, 1))
+    dims = (n_rows, n_cols, tile_rows, tile_cols, half, pixels, near_slots, far_slots, served)
+    block = (half, pixels)
+    bf16, f32, i32 = jnp.bfloat16, jnp.float32, jnp.int32
+    all_rows = tile_rows * tile_cols * half
+    group_rows = tile_rows * half * max([n_rows * served] + [2 * size for size in sizes])
+    dma = pltpu.SemaphoreType.DMA
+    scratch = [pltpu.VMEM((n_rows * tile_rows, size) + block, bf16) for size in sizes]
+    scratch += [
+        pltpu.VMEM((n_rows * tile_rows, served) + block, bf16),
+        pltpu.VMEM((tile_rows + 4, tile_cols + 4) + block, bf16),
+        pltpu.VMEM((tile_rows, served) + block, bf16),
+        pltpu.VMEM((2,) + near_factor.shape, bf16),
+        pltpu.VMEM((2,) + far_factor.shape, bf16),
+        pltpu.VMEM((2,) + near_codes.shape, i32),
+        pltpu.VMEM((n_rows, 2) + far_codes.shape, i32),
+        pltpu.SMEM((2,) + near_codes.shape, i32),
+        pltpu.SMEM((n_rows, 2) + far_codes.shape, i32),
+        pltpu.SMEM(block_level.shape, i32),
+        pltpu.VMEM((all_rows, 2 * near_slots // PARTS * pixels), bf16),
+        pltpu.VMEM((group_rows, 2 * far_slots * pixels), bf16),
+        pltpu.VMEM((all_rows, pixels), f32),
+        pltpu.VMEM((group_rows, pixels), f32),
+        pltpu.VMEM((3, tile_rows, served) + block, bf16),
+        pltpu.VMEM((tile_rows, tile_cols - 2 * served) + block, bf16),
+        pltpu.VMEM((tile_rows, tile_cols) + block, bf16),
+        dma((26 + 4 * len(sizes),)),
+        dma((26 + 4 * len(sizes),)),
+        dma((16 + 3 * len(sizes),)),
+    ]
+    anywhere = pl.BlockSpec(memory_space=pl.ANY)
+    vmem = pl.BlockSpec(memory_space=pltpu.VMEM)
+    white = pl.pallas_call(
+        functools.partial(pair_kernel, dims),
+        out_shape=pltpu.VMEM((tile_rows, tile_cols) + block, bf16),
+        in_specs=[anywhere] * 6,
+        out_specs=vmem,
+        scratch_shapes=scratch,
+        compiler_params=pltpu.CompilerParams(
+            collective_id=0, has_side_effects=True, vmem_limit_bytes=56 * 1024 * 1024),
+    )(convergence, near_codes, far_codes, block_level, near_factor, far_factor)
+    return pl.pallas_call(
+        put_out,
+        out_shape=jax.ShapeDtypeStruct(white.shape, bf16),
+        in_specs=[vmem],
+        out_specs=anywhere,
+        scratch_shapes=[dma((tile_rows,))],
+    )(pltpu.with_memory_space_constraint(white, pltpu.VMEM))
+
+
 def solution(mesh):
     placed = (
         P(("fields", "rows"), "cols", None, None),
@@ -497,8 +1027,9 @@
         P(None, "sub"),
         P(None, "sub"),
     )
+    two_middle_tiles = mesh.shape["rows"] - 2 == 2
     return jax.shard_map(
-        on_device,
+        pair_on_device if two_middle_tiles else on_device,
         mesh=mesh,
         in_specs=placed,
         out_specs=P(("fields", "rows"), "cols", "sub", None),

time: 42.4 us -> 36.9 us (0.87)
  Pallas kernels: 38.9 us -> 36.8 us
  local copies, waits for them, and re-layouts: 1.87 us -> 0 us
  other arithmetic: 1.34 us -> 0 us
    pallas_call x1 -> x2, Pallas kernels: 38.9 us -> 36.8 us  [the longest x1 36 us: pair_on_device(): pl.pallas_call(functools.partial(pair_kernel, dims), out_shape=pltpu.VMEM...]
    unnamed x1 -> x0, local copies, waits for them, and re-layouts: 1.87 us -> none
    concatenate x1 -> x0, other arithmetic: 1.34 us -> none  [on_device(): jnp.concatenate([jnp.transpose(near_codes, (0, 2, 1)), jnp.transpose(far_...]
where the time goes in v1:
time: 36.9 us; the launch traced here: 36.8 us
  Pallas kernels  36.8 us (100%)
    pallas_call x1, Pallas kernels, pair_on_device(): pl.pallas_call(functools.partial(pair_kernel, dims), out_shape=pltpu.VMEM...  36 us
    pallas_call x1, Pallas kernels, pair_on_device(): pl.pallas_call(put_out, out_shape=jax.ShapeDtypeStruct(white.shape, bf16)...  0.82 us

profile of v1, /device:TPU:0, one launch (start us, length us, event | category | flops | bytes accessed | tf_op | source)
XLA Modules:
  0.0 36.8 jit_solution(14292659078215946638)
XLA Ops:
  0.0 36.0 %shard_map.64.src = bf16[4,16,8,512]{3,2,1,0:T(8,128)(2,1)S(1)} custom-call(bf16[4,16,16,512]{3,2,1,0:T(8,128)(2,1)} %conv.1, s32[4,4,16]{2,1,0:T(4,128)} %bitcast.2, s32[4,2,16]{2,1,0:T(2,128)} %bitcast.3, s32[4,16]{1,0:T(4,128)} %levels.1, bf16[512,2048]{1,0:T(8,128)(2,1)} %near_factor.1, bf16[512,1024]{1,0:T(8,128)(2,1)} %far_factor.1), custom_call_target="tpu_custom_call" | custom-call | tf_op jit(solution)/shard_map/pallas_call | solution.py:1003
  36.0 0.8 %shard_map.65 = bf16[4,16,8,512]{3,2,1,0:T(8,128)(2,1)} custom-call(bf16[4,16,8,512]{3,2,1,0:T(8,128)(2,1)S(1)} %shard_map.64.src), custom_call_target="tpu_custom_call" | custom-call | tf_op jit(solution)/shard_map/pallas_call | solution.py:1012

commit v2 on v1

--- a/solution.py
+++ b/solution.py
@@ -499,8 +499,8 @@
     chunks = len(starts) - 1
     sizes = [starts[k + 1] - starts[k] for k in range(chunks)]
     far_both = scratch[:chunks]
-    (far_served, near, stage, near_w, far_w, near_codes_v, far_codes_v, near_codes_s, far_codes_s, levels_s,
-     near_g, far_g, near_acc, far_acc, white_served, white_both, white_in, send_sem, recv_sem, loc_sem) = scratch[chunks:]
+    (far_served, near, stage, bits, near_w, far_w, near_codes_v, far_codes_v, near_codes_s, far_codes_s, levels_s,
+     near_g, far_g, near_acc, far_acc, white_served, white_both, white_own, white_in, send_sem, recv_sem, loc_sem) = scratch[chunks:]
 
     i = lax.axis_index("rows")
     x = lax.axis_index("cols")
@@ -641,7 +641,7 @@
 
     from_inside = pl.ds(jnp.where(low, above, below), edge)
     from_outside = pl.ds(jnp.where(low, below, above), edge)
-    edge_rows = conv.at[pl.ds(in_edge, edge), :, mine, :]
+    late_cols = pl.ds(starts[1], tile_cols - starts[1])
 
     code_near = exchange(near_codes, near_codes_v.at[s], near_codes_v.at[other])
     code_own = between(far_codes, far_codes_v.at[i, s], far_codes_v.at[i, other])
@@ -653,41 +653,44 @@
         for tile in (end, far_mid, far_end)
     ]
 
-    mid_edge = across(edge_rows, near.at[from_outside, inner], near.at[from_inside, inner])
-    end_edge = inward(edge_rows, near.at[from_outside, inner], near.at[from_outside, inner])
+    def halo(rows, first, size):
+        return near.at[rows, pl.ds(edge + first, size)]
+
+    def in_edge_of(cols):
+        return conv.at[pl.ds(in_edge, edge), cols, mine, :]
+
+    def all_rows_of(cols):
+        return conv.at[:, cols, mine, :]
+
+    def tile_of(ref, tile):
+        return ref.at[rows_of(tile, 0, tile_rows)]
+
     back_edge = outward(
         conv.at[pl.ds(out_edge, edge), :, mine, :], near.at[from_inside, inner], near.at[from_inside, inner])
-
-    their_rest = pl.ds(jnp.where(low, edge, 0), rest)
-
-    def rest_of(cols):
-        return conv.at[pl.ds(in_rest, rest), cols, mine, :]
-
-    def far_mid_rest(ref):
-        return ref.at[pl.ds(far_mid * tile_rows + jnp.where(low, edge, 0), rest)]
-
-    mid_rest = across(
-        rest_of(theirs_cols), far_served.at[rows_of(mid, in_rest, rest)], far_mid_rest(far_served))
-    mid_rest_both = [
-        across(rest_of(both_cols(k)), far_both[k].at[rows_of(mid, in_rest, rest)], far_mid_rest(far_both[k]))
-        for k in range(chunks)
-    ]
-
-    def end_rest_to(cols, ref):
-        return inward(rest_of(cols), ref, ref)
-
-    end_rest_theirs = end_rest_to(theirs_cols, stage.at[pl.ds(in_rest, rest)])
-    end_rest_both = [
-        end_rest_to(both_cols(k), far_both[k].at[rows_of(end, in_rest, rest)]) for k in range(chunks)
-    ]
-    end_rest_served = end_rest_to(served_cols, far_served.at[rows_of(end, in_rest, rest)])
-
-    relay_theirs = across(
-        stage, far_served.at[rows_of(end, 0, tile_rows)], far_served.at[rows_of(far_end, 0, tile_rows)])
+    mid_theirs = across(all_rows_of(theirs_cols), tile_of(far_served, mid), tile_of(far_served, far_mid))
+    mid_first = across(all_rows_of(both_cols(0)), tile_of(far_both[0], mid), tile_of(far_both[0], far_mid))
+    edge_served = across(
+        in_edge_of(served_cols), halo(from_outside, served_at, served), halo(from_inside, theirs_at, served))
+    edge_late = across(
+        in_edge_of(late_cols), halo(from_outside, late_cols.start, late_cols.size),
+        halo(from_inside, late_cols.start, late_cols.size))
+    their_rest = jnp.where(low, edge, 0)
+    mid_rest = [
+        across(
+            conv.at[pl.ds(in_rest, rest), both_cols(k), mine, :], far_both[k].at[rows_of(mid, in_rest, rest)],
+            far_both[k].at[rows_of(far_mid, their_rest, rest)])
+        for k in range(1, chunks)
+    ]
+
+    def end_to(cols, ref):
+        return inward(all_rows_of(cols), ref, ref)
+
+    end_theirs = end_to(theirs_cols, stage)
+    end_served = end_to(served_cols, tile_of(far_served, end))
+    end_both = [end_to(both_cols(k), tile_of(far_both[k], end)) for k in range(chunks)]
+    relay_theirs = across(stage, tile_of(far_served, end), tile_of(far_served, far_end))
     relay_both = [
-        across(
-            far_both[k].at[rows_of(end, 0, tile_rows)], far_both[k].at[rows_of(end, 0, tile_rows)],
-            far_both[k].at[rows_of(far_end, 0, tile_rows)])
+        across(tile_of(far_both[k], end), tile_of(far_both[k], end), tile_of(far_both[k], far_end))
         for k in range(chunks)
     ]
 
@@ -710,85 +713,93 @@
 
     sides = [side_copy(dx) for dx in (-1, 1)]
 
+    def bit_of(di, dx):
+        return bits.at[di + 1 + (dx + 1) // 2]
+
+    def bit_copy(di, dx):
+        src = conv.at[
+            pl.ds(0 if di == -1 else tile_rows - edge, edge), pl.ds(0 if dx == -1 else tile_cols - edge, edge), mine, :]
+        return Remote(
+            present(di, 0) & present(0, dx), present(-di, 0) & present(0, dx), src, bit_of(-di, dx), bit_of(-di, dx),
+            {"rows": i + di})
+
     def corner_copy(di, dx):
-        rows = pl.ds(below if di == -1 else above, edge)
-        src, dst = (edge, tile_cols + edge) if dx == -1 else (tile_cols, 0)
-        at = near.at[rows, pl.ds(dst, edge)]
+        at = near.at[pl.ds(below if di == -1 else above, edge), pl.ds(tile_cols + edge if dx == -1 else 0, edge)]
         return Remote(
-            present(di, 0) & present(0, dx), present(di, 0) & present(0, -dx), near.at[rows, pl.ds(src, edge)], at, at,
-            {"cols": x + dx})
-
-    corners = [corner_copy(di, dx) for di in (-1, 1) for dx in (-1, 1)]
+            present(di, 0) & present(0, dx), present(di, 0) & present(0, -dx), bit_of(di, dx), at, at, {"cols": x + dx})
+
+    diagonals = [(di, dx) for di in (-1, 1) for dx in (-1, 1)]
+    bit_flows = {(-di, dx): bit_copy(di, dx) for di, dx in diagonals}
+    corners = {(di, dx): corner_copy(di, dx) for di, dx in diagonals}
     factor_near = exchange(near_factor, near_w.at[s], near_w.at[other])
     factor_far = between(far_factor, far_w.at[s], far_w.at[other])
 
-    end_to_far = [
-        Local(is_mid, near.at[from_outside, pl.ds(edge + theirs_at, served)], stage.at[pl.ds(in_edge, edge)]),
-        Local(is_mid, near.at[from_outside, pl.ds(edge + served_at, served)], far_served.at[rows_of(end, in_edge, edge)]),
+    their_edge = jnp.where(low, 0, tile_rows - edge)
+    end_halos = [
+        Local(is_mid, stage.at[pl.ds(in_edge, edge)], halo(from_outside, theirs_at, served)),
+        Local(is_mid, far_served.at[rows_of(end, in_edge, edge)], halo(from_outside, served_at, served)),
     ] + [
-        Local(
-            is_mid, near.at[from_outside, pl.ds(edge + starts[k], sizes[k])],
-            far_both[k].at[rows_of(end, in_edge, edge)])
+        Local(is_mid, far_both[k].at[rows_of(end, in_edge, edge)], halo(from_outside, starts[k], sizes[k]))
         for k in range(chunks)
     ]
-    their_edge = jnp.where(low, 0, tile_rows - edge)
-    mid_to_far = [
-        Local(
-            is_mid, near.at[from_inside, pl.ds(edge + served_at, served)],
-            far_served.at[pl.ds(far_mid * tile_rows + their_edge, edge)]),
-    ] + [
-        Local(
-            is_mid, near.at[from_inside, pl.ds(edge + starts[k], sizes[k])],
-            far_both[k].at[pl.ds(far_mid * tile_rows + their_edge, edge)])
-        for k in range(chunks)
+    mid_halos = [
+        Local(is_mid, far_served.at[rows_of(far_mid, their_edge, edge)], halo(from_inside, served_at, served)),
+        Local(is_mid, far_both[0].at[rows_of(far_mid, their_edge, edge)], halo(from_inside, starts[0], sizes[0])),
+    ]
+    late_edges = [
+        Local(is_mid, halo(from_inside, starts[k], sizes[k]), far_both[k].at[rows_of(far_mid, their_edge, edge)])
+        for k in range(1, chunks)
     ]
     near_codes_in = Local(always, near_codes_v.at[other], near_codes_s.at[other])
     far_codes_in = [Local(is_mid, far_codes_v.at[i, other], far_codes_s.at[i, other])] + [
         Local(is_mid, far_codes_v.at[tile], far_codes_s.at[tile]) for tile in (end, far_mid, far_end)
     ]
 
-    first = [code_end, code_mid, code_near, code_own, mid_edge, end_edge, back_edge] + sides + [factor_near, factor_far]
-    for flow in first:
+    small = [code_end, code_mid] + [bit_flows[d] for d in diagonals] + [code_near, code_own]
+    large = [mid_theirs, end_theirs, mid_first, end_both[0], back_edge, end_served] + end_both[1:]
+    factors = [factor_far, factor_near]
+    for flow in small + large + sides + factors:
         flow.start()
-    end_rest_theirs.start()
-    for k in range(chunks):
-        end_rest_both[k].start()
-    end_rest_served.start()
     code_end.wait_recv()
     code_relay.start()
-    mid_rest.start()
-    for k in range(chunks):
-        mid_rest_both[k].start()
     code_share[0].start()
+    for d in diagonals:
+        bit_flows[d].wait_recv()
+        corners[d].start()
     code_mid.wait_recv()
     code_share[1].start()
     code_near.wait_recv()
     near_codes_in.start()
     code_own.wait_recv()
     far_codes_in[0].start()
-
-    end_edge.wait_recv()
-    for copy in end_to_far:
-        copy.start()
-    mid_edge.wait_recv()
-    back_edge.wait_recv()
-    own[0].wait()
-    for corner in corners:
-        corner.start()
-    for copy in mid_to_far:
-        copy.start()
-    for copy in own[1:]:
+    for copy in own:
         copy.wait()
-    for copy in end_to_far:
-        copy.wait()
-    end_rest_theirs.wait_recv()
-    relay_theirs.start()
     near_codes_in.wait()
     for side in sides:
         side.wait_recv()
-    factor_near.wait_recv()
-    for corner in corners:
-        corner.wait_recv()
+    for d in diagonals:
+        corners[d].wait_recv()
+
+    end_theirs.wait_recv()
+    relay_theirs.start()
+    end_halos[0].start()
+    end_both[0].wait_recv()
+    relay_both[0].start()
+    edge_served.start()
+    edge_late.start()
+    for flow in mid_rest:
+        flow.start()
+    end_halos[2].start()
+    code_relay.wait_recv()
+    code_share[2].start()
+    for share in code_share:
+        share.wait_recv()
+    for copy in far_codes_in[1:]:
+        copy.start()
+    for copy in far_codes_in:
+        copy.wait()
+    for factor in factors:
+        factor.wait_recv()
 
     contract = (((1,), (1,)), ((), ()))
     part_slots = 2 * near_slots // PARTS
@@ -866,7 +877,7 @@
 
     def put_own(col0):
         def put(r, c, white):
-            out[r, col0 + c] = jnp.where(levels_s[r, col0 + c] == 1, fine(r, col0 + c), white).astype(jnp.bfloat16)
+            white_own[r, col0 + c] = white.astype(jnp.bfloat16)
         return put
 
     def put_served(which):
@@ -879,69 +890,81 @@
             white_both[r, col0 - starts[0] + c] = white.astype(jnp.bfloat16)
         return put
 
-    def finish(first, last):
+    def finish(first, last, whites):
         def body(c, carry):
             for r in range(tile_rows):
-                white = white_in[r, c].astype(jnp.float32)
+                white = whites[r, c].astype(jnp.float32)
                 out[r, c] = jnp.where(levels_s[r, c] == 1, fine(r, c), white).astype(jnp.bfloat16)
             return carry
 
         lax.fori_loop(first, last, body, 0)
 
+    def far_late(k):
+        mid_rest[k - 1].wait_recv()
+        relay_both[k].wait_recv()
+        late_edges[k - 1].wait()
+        far_group(far_both[k], starts[k], sizes[k], [(end, put_both(starts[k])), (i, put_own(starts[k]))])
+        white_end_both[k].start()
+
     @pl.when(is_mid)
     def _():
-        near_part(0)
-        code_relay.wait_recv()
-        code_share[2].start()
-        near_part(1)
-        for copy in mid_to_far:
-            copy.wait()
-        for k in range(chunks):
-            end_rest_both[k].wait_recv()
-            relay_both[k].start()
-        for k in range(2, PARTS):
-            near_part(k)
-        for share in code_share:
-            share.wait_recv()
-        for copy in far_codes_in[1:]:
-            copy.start()
-        for copy in far_codes_in:
-            copy.wait()
-        factor_far.wait_recv()
-        mid_rest.wait_recv()
-        end_rest_served.wait_recv()
+        mid_theirs.wait_recv()
+        end_served.wait_recv()
         relay_theirs.wait_recv()
+        end_halos[1].start()
+        mid_halos[0].start()
         far_group(far_served, served_at, served, [
             (far_end, put_served(2)), (far_mid, put_served(1)), (end, put_served(0)), (i, put_own(served_at))])
+        white_end.start()
+        mid_first.wait_recv()
+        relay_both[0].wait_recv()
+        mid_halos[1].start()
+        far_group(far_both[0], starts[0], sizes[0], [(end, put_both(starts[0])), (i, put_own(starts[0]))])
+        white_end_both[0].start()
+        for k in range(1, chunks):
+            end_both[k].wait_recv()
+            relay_both[k].start()
+            end_halos[2 + k].start()
         white_far_end.start()
         white_far_mid.start()
-        white_end.start()
-        for k in range(chunks):
-            mid_rest_both[k].wait_recv()
-            relay_both[k].wait_recv()
-            far_group(far_both[k], starts[k], sizes[k], [(end, put_both(starts[k])), (i, put_own(starts[k]))])
-            white_end_both[k].start()
+        edge_served.wait_recv()
+        edge_late.wait_recv()
+        for copy in late_edges:
+            copy.start()
+        for copy in end_halos + mid_halos:
+            copy.wait()
+        near_part(0)
+        near_part(1)
+        for k in range(1, chunks):
+            far_late(k)
+        near_part(2)
+        near_part(3)
+        finish(served_at, served_at + served, white_own)
+        finish(starts[0], tile_cols, white_own)
         white_far_mid.wait_recv()
-        finish(theirs_at, theirs_at + served)
+        finish(theirs_at, theirs_at + served, white_in)
 
     @pl.when(is_end)
     def _():
+        back_edge.wait_recv()
         for part in range(PARTS):
             near_part(part)
         white_end.wait_recv()
-        finish(served_at, served_at + served)
+        finish(served_at, served_at + served, white_in)
         for k in range(chunks - 1):
             white_end_both[k].wait_recv()
-            finish(starts[k], starts[k + 1])
+            finish(starts[k], starts[k + 1], white_in)
         white_far_end.wait_recv()
-        finish(theirs_at, theirs_at + served)
+        finish(theirs_at, theirs_at + served, white_in)
         white_end_both[chunks - 1].wait_recv()
-        finish(starts[chunks - 1], starts[chunks])
-
-    for flow in first + [end_rest_theirs] + end_rest_both + [end_rest_served, code_relay, mid_rest] + mid_rest_both:
+        finish(starts[chunks - 1], starts[chunks], white_in)
+
+    for flow in small + large + sides + factors + [code_relay] + code_share:
         flow.wait_send()
-    for flow in corners + [relay_theirs] + relay_both + code_share:
+    for flow in [relay_theirs, edge_served, edge_late] + relay_both + mid_rest:
         flow.wait_send()
+    for d in diagonals:
+        corners[d].wait_send()
     for flow in [white_far_end, white_far_mid, white_end] + white_end_both:
         flow.wait_send()
 
@@ -980,6 +1003,7 @@
         pltpu.VMEM((n_rows * tile_rows, served) + block, bf16),
         pltpu.VMEM((tile_rows + 4, tile_cols + 4) + block, bf16),
         pltpu.VMEM((tile_rows, served) + block, bf16),
+        pltpu.VMEM((4, 2, 2) + block, bf16),
         pltpu.VMEM((2,) + near_factor.shape, bf16),
         pltpu.VMEM((2,) + far_factor.shape, bf16),
         pltpu.VMEM((2,) + near_codes.shape, i32),
@@ -994,8 +1018,9 @@
         pltpu.VMEM((3, tile_rows, served) + block, bf16),
         pltpu.VMEM((tile_rows, tile_cols - 2 * served) + block, bf16),
         pltpu.VMEM((tile_rows, tile_cols) + block, bf16),
-        dma((26 + 4 * len(sizes),)),
-        dma((26 + 4 * len(sizes),)),
+        pltpu.VMEM((tile_rows, tile_cols) + block, bf16),
+        dma((30 + 4 * len(sizes),)),
+        dma((30 + 4 * len(sizes),)),
         dma((16 + 3 * len(sizes),)),
     ]
     anywhere = pl.BlockSpec(memory_space=pl.ANY)

time: 36.9 us -> 33 us (0.89)
  Pallas kernels: 36.8 us -> 32.8 us
    pallas_call x1, Pallas kernels: 36 us -> 32 us  [pair_on_device(): pl.pallas_call(functools.partial(pair_kernel, dims), out_shape=pltpu.VMEM...]
where the time goes in v2:
time: 33 us; the launch traced here: 32.8 us
  Pallas kernels  32.8 us (99%)
    pallas_call x1, Pallas kernels, pair_on_device(): pl.pallas_call(functools.partial(pair_kernel, dims), out_shape=pltpu.VMEM...  32 us
    pallas_call x1, Pallas kernels, pair_on_device(): pl.pallas_call(put_out, out_shape=jax.ShapeDtypeStruct(white.shape, bf16)...  0.82 us

profile of v2, /device:TPU:0, one launch (start us, length us, event | category | flops | bytes accessed | tf_op | source)
XLA Modules:
  0.0 32.8 jit_solution(16567265486720545886)
XLA Ops:
  0.0 32.0 %shard_map.64.src = bf16[4,16,8,512]{3,2,1,0:T(8,128)(2,1)S(1)} custom-call(bf16[4,16,16,512]{3,2,1,0:T(8,128)(2,1)} %conv.1, s32[4,4,16]{2,1,0:T(4,128)} %bitcast.2, s32[4,2,16]{2,1,0:T(2,128)} %bitcast.3, s32[4,16]{1,0:T(4,128)} %levels.1, bf16[512,2048]{1,0:T(8,128)(2,1)} %near_factor.1, bf16[512,1024]{1,0:T(8,128)(2,1)} %far_factor.1), custom_call_target="tpu_custom_call" | custom-call | tf_op jit(solution)/shard_map/pallas_call | solution.py:1028
  32.0 0.8 %shard_map.65 = bf16[4,16,8,512]{3,2,1,0:T(8,128)(2,1)} custom-call(bf16[4,16,8,512]{3,2,1,0:T(8,128)(2,1)S(1)} %shard_map.64.src), custom_call_target="tpu_custom_call" | custom-call | tf_op jit(solution)/shard_map/pallas_call | solution.py:1037

commit v3 on v2

--- a/solution.py
+++ b/solution.py
@@ -775,17 +775,11 @@
     for copy in own:
         copy.wait()
     near_codes_in.wait()
-    for side in sides:
-        side.wait_recv()
-    for d in diagonals:
-        corners[d].wait_recv()
-
     end_theirs.wait_recv()
     relay_theirs.start()
     end_halos[0].start()
     end_both[0].wait_recv()
     relay_both[0].start()
-    edge_served.start()
     edge_late.start()
     for flow in mid_rest:
         flow.start()
@@ -801,6 +795,12 @@
     for factor in factors:
         factor.wait_recv()
 
+    def beside():
+        for side in sides:
+            side.wait_recv()
+        for d in diagonals:
+            corners[d].wait_recv()
+
     contract = (((1,), (1,)), ((), ()))
     part_slots = 2 * near_slots // PARTS
 
@@ -899,6 +899,14 @@
 
         lax.fori_loop(first, last, body, 0)
 
+    def early_sends():
+        for flow in small + large + sides + factors + [corners[d] for d in diagonals]:
+            flow.wait_send()
+
+    def relay_sends():
+        for flow in [code_relay, relay_theirs, edge_served, edge_late] + code_share + relay_both + mid_rest:
+            flow.wait_send()
+
     def far_late(k):
         mid_rest[k - 1].wait_recv()
         relay_both[k].wait_recv()
@@ -916,39 +924,45 @@
         far_group(far_served, served_at, served, [
             (far_end, put_served(2)), (far_mid, put_served(1)), (end, put_served(0)), (i, put_own(served_at))])
         white_end.start()
+        for k in range(1, chunks):
+            end_both[k].wait_recv()
+            relay_both[k].start()
+            end_halos[2 + k].start()
         mid_first.wait_recv()
         relay_both[0].wait_recv()
         mid_halos[1].start()
         far_group(far_both[0], starts[0], sizes[0], [(end, put_both(starts[0])), (i, put_own(starts[0]))])
         white_end_both[0].start()
-        for k in range(1, chunks):
-            end_both[k].wait_recv()
-            relay_both[k].start()
-            end_halos[2 + k].start()
+        edge_served.start()
         white_far_end.start()
         white_far_mid.start()
-        edge_served.wait_recv()
         edge_late.wait_recv()
         for copy in late_edges:
             copy.start()
+        for k in range(1, chunks):
+            far_late(k)
+        edge_served.wait_recv()
         for copy in end_halos + mid_halos:
             copy.wait()
-        near_part(0)
-        near_part(1)
-        for k in range(1, chunks):
-            far_late(k)
-        near_part(2)
-        near_part(3)
+        beside()
+        for part in range(PARTS):
+            near_part(part)
         finish(served_at, served_at + served, white_own)
         finish(starts[0], tile_cols, white_own)
+        early_sends()
+        relay_sends()
         white_far_mid.wait_recv()
         finish(theirs_at, theirs_at + served, white_in)
+        for flow in [white_far_end, white_far_mid, white_end] + white_end_both:
+            flow.wait_send()
 
     @pl.when(is_end)
     def _():
         back_edge.wait_recv()
+        beside()
         for part in range(PARTS):
             near_part(part)
+        early_sends()
         white_end.wait_recv()
         finish(served_at, served_at + served, white_in)
         for k in range(chunks - 1):
@@ -958,15 +972,6 @@
         finish(theirs_at, theirs_at + served, white_in)
         white_end_both[chunks - 1].wait_recv()
         finish(starts[chunks - 1], starts[chunks], white_in)
-
-    for flow in small + large + sides + factors + [code_relay] + code_share:
-        flow.wait_send()
-    for flow in [relay_theirs, edge_served, edge_late] + relay_both + mid_rest:
-        flow.wait_send()
-    for d in diagonals:
-        corners[d].wait_send()
-    for flow in [white_far_end, white_far_mid, white_end] + white_end_both:
-        flow.wait_send()
 
 
 def put_out(src, dst, sem):

time: 33 us -> 32.9 us (level)
  no operation moved by 1% of the time
where the time goes in v3:
time: 32.9 us; the launch traced here: 32.8 us
  Pallas kernels  32.8 us (100%)
    pallas_call x1, Pallas kernels, pair_on_device(): pl.pallas_call(functools.partial(pair_kernel, dims), out_shape=pltpu.VMEM...  32 us
    pallas_call x1, Pallas kernels, pair_on_device(): pl.pallas_call(put_out, out_shape=jax.ShapeDtypeStruct(white.shape, bf16)...  0.82 us

profile of v3, /device:TPU:0, one launch (start us, length us, event | category | flops | bytes accessed | tf_op | source)
XLA Modules:
  0.0 32.8 jit_solution(17866561175665676547)
XLA Ops:
  0.0 32.0 %shard_map.64.src = bf16[4,16,8,512]{3,2,1,0:T(8,128)(2,1)S(1)} custom-call(bf16[4,16,16,512]{3,2,1,0:T(8,128)(2,1)} %conv.1, s32[4,4,16]{2,1,0:T(4,128)} %bitcast.2, s32[4,2,16]{2,1,0:T(2,128)} %bitcast.3, s32[4,16]{1,0:T(4,128)} %levels.1, bf16[512,2048]{1,0:T(8,128)(2,1)} %near_factor.1, bf16[512,1024]{1,0:T(8,128)(2,1)} %far_factor.1), custom_call_target="tpu_custom_call" | custom-call | tf_op jit(solution)/shard_map/pallas_call | solution.py:1033
  32.0 0.8 %shard_map.65 = bf16[4,16,8,512]{3,2,1,0:T(8,128)(2,1)} custom-call(bf16[4,16,8,512]{3,2,1,0:T(8,128)(2,1)S(1)} %shard_map.64.src), custom_call_target="tpu_custom_call" | custom-call | tf_op jit(solution)/shard_map/pallas_call | solution.py:1042
